TPU v7x, 32 devices: a whole 2x2x4 slice. The times are simulated.
32 devices in a mesh: dp: 8 (over y, x, core), tensor: 4 (over z).
Axes of the slice: x: 2, y: 2, z: 4, core: 2. Of those that a mesh axis runs over, the one named last changes fastest.
Arguments:
- language: bfloat16 [256, 20, 768], P(('dp', 'tensor')), may hold values from -6 to 6
- visual: bfloat16 [256, 36, 768], P(('dp', 'tensor')), may hold values from -6 to 6
- word_count: int32 [256], P('dp'), may hold values from 5 to 20
- region_count: int32 [256], P('dp'), may hold values from 10 to 36
- task_flags: int32 [256, 3], P(('dp', 'tensor')), may hold values 0 or 1
- grad_language: bfloat16 [256, 20, 768], P(('dp', 'tensor')), may hold values from -6 to 6
- grad_visual: bfloat16 [256, 36, 768], P(('dp', 'tensor')), may hold values from -6 to 6
- cross_project: bfloat16 [3, 768, 768], P(None, None, 'tensor'), may hold values from -0.21875 to 0.21875
- cross_bias: float32 [2, 768], P(None, 'tensor'), may hold values from -2 to 2
- cross_out: bfloat16 [768, 768], P('tensor'), may hold values from -0.625 to 0.625
- cross_out_bias: float32 [768], replicated, may hold values from -2 to 2
- cross_gain: float32 [768], replicated, may hold values from 0.5 to 1.5
- cross_shift: float32 [768], replicated, may hold values from -2 to 2
- self_project: bfloat16 [2, 3, 768, 768], P(None, None, None, 'tensor'), may hold values from -0.21875 to 0.21875
- self_bias: float32 [2, 2, 768], P(None, None, 'tensor'), may hold values from -2 to 2
- self_out: bfloat16 [2, 768, 768], P(None, 'tensor'), may hold values from -0.625 to 0.625
- self_out_bias: float32 [2, 768], replicated, may hold values from -2 to 2
- self_gain: float32 [2, 768], replicated, may hold values from 0.5 to 1.5
- self_shift: float32 [2, 768], replicated, may hold values from -2 to 2
- feed_in: bfloat16 [2, 768, 3072], P(None, None, 'tensor'), may hold values from -0.21875 to 0.21875
- feed_in_bias: float32 [2, 3072], P(None, 'tensor'), may hold values from -2 to 2
- feed_out: bfloat16 [2, 3072, 768], P(None, 'tensor'), may hold values from -0.15625 to 0.15625
- feed_out_bias: float32 [2, 768], replicated, may hold values from -2 to 2
- feed_gain: float32 [2, 768], replicated, may hold values from 0.5 to 1.5
- feed_shift: float32 [2, 768], replicated, may hold values from -2 to 2
Outputs:
- language_out: bfloat16 [256, 20, 768], P(('dp', 'tensor'))
- visual_out: bfloat16 [256, 36, 768], P(('dp', 'tensor'))
- grad_language_in: float32 [256, 20, 768], P(('dp', 'tensor'))
- grad_visual_in: float32 [256, 36, 768], P(('dp', 'tensor'))
- grad_cross_project: float32 [3, 768, 768], P(None, 'dp', 'tensor')
- grad_cross_bias: float32 [2, 768], replicated
- grad_cross_out: float32 [768, 768], P('tensor', 'dp')
- grad_cross_out_bias: float32 [768], replicated
- grad_cross_gain: float32 [768], replicated
- grad_cross_shift: float32 [768], replicated
- grad_self_project: float32 [2, 3, 768, 768], P(None, None, 'dp', 'tensor')
- grad_self_bias: float32 [2, 2, 768], replicated
- grad_self_out: float32 [2, 768, 768], P(None, 'tensor', 'dp')
- grad_self_out_bias: float32 [2, 768], replicated
- grad_self_gain: float32 [2, 768], replicated
- grad_self_shift: float32 [2, 768], replicated
- grad_feed_in: float32 [2, 768, 3072], P(None, 'dp', 'tensor')
- grad_feed_in_bias: float32 [2, 3072], replicated
- grad_feed_out: float32 [2, 3072, 768], P(None, 'tensor', 'dp')
- grad_feed_out_bias: float32 [2, 768], replicated
- grad_feed_gain: float32 [2, 768], replicated
- grad_feed_shift: float32 [2, 768], replicated
Inputs may be any that keep to these rules, and one draw needn't show every extreme that they name: `word_count`: slots at positions >= the count are padding: no query attends to them. `region_count`: slots at positions >= the count are padding: no query attends to them. `task_flags`: column 0: masked word prediction, column 1: VQA answer, column 2: GQA answer.
All inputs are finite; a program needn't handle non-finite values. No bound on the sum of `task_flags` on one device may be relied on, other than what follows from the above.
Results may differ from a plain program's by a relative error of at most 0.025.
Values may be sent and summed in bfloat16 or wider, within the bound.
A program may use at most 192 MiB of HBM per device.

v0:
```python
import functools

import jax
import jax.numpy as jnp
from jax import lax
from jax.experimental import pallas as pl
from jax.experimental.pallas import tpu as pltpu
from jax.sharding import PartitionSpec as P

D = 768
HEAD_DIM = 64
LAYER_EPS = 1e-06
MASKED = -1e30
GROUP = 8
MESH = pl.DeviceIdType.MESH
BF = jnp.bfloat16
F32 = jnp.float32


def place():
    dp = lax.axis_index("dp")
    z = lax.axis_index("tensor")
    core = dp % 2
    bx = (dp // 2) % 2
    by = (dp // 4) % 2
    return dp, z, core, bx, by


def greet(targets):
    barrier = pltpu.get_barrier_semaphore()
    count = 0
    for device, valid in targets:
        if valid is None:
            pl.semaphore_signal(barrier, inc=1, device_id=device, device_id_type=MESH)
            count = count + 1
        else:

            @pl.when(valid)
            def _(device=device):
                pl.semaphore_signal(barrier, inc=1, device_id=device, device_id_type=MESH)

            count = count + valid.astype(jnp.int32)
    pl.semaphore_wait(barrier, count)


K_Z, K_X, K_Y, K_A, K_B, K_C, K_Z2 = 0, 1, 2, 3, 4, 5, 10
TILE = 256


def gather_steps(nz, units, whole, send_sem, recv_sem):
    dp, z, core, bx, by = place()
    low = dp % GROUP
    dev_c = (dp + 1 - 2 * core, z)
    dev_x = (dp + 2 - 4 * bx, z)
    dev_y = (dp + 4 - 8 * by, z)
    sl_x = low + 2 - 4 * bx
    sl_y = low + 4 - 8 * by
    sl_d = low + 2 - 4 * bx + 4 - 8 * by

    def copy(src, dst, u, k, kind, device):
        return pltpu.make_async_remote_copy(
            src_ref=src, dst_ref=dst, send_sem=send_sem.at[u, k, kind], recv_sem=recv_sem.at[u, k, kind], device_id=device, device_id_type=MESH
        )

    def is_attention(u):
        return len(units[u]) == 2

    def part(u, j, sl, half):
        if is_attention(u):
            size = units[u][1].shape[0]
            step = size // GROUP
            rows = pl.ds(pl.multiple_of(j * size + sl * step, 8), step)
            return whole[u].at[:, rows] if half is None else whole[u].at[2 * half : 2 * half + 2, rows]
        step = units[u][0].shape[0] // GROUP
        if half is None:
            return whole[u].at[j, pl.ds(pl.multiple_of(sl * step, 8), step)]
        return whole[u].at[j, pl.ds(pl.multiple_of(sl * step + half * (step // 2), 8), step // 2)]

    def z_copies(u, k, j, device, sending):
        if is_attention(u):
            proj, out = units[u]
            size = out.shape[0]
            step = size // GROUP
            mine = pl.ds(pl.multiple_of(low * step, 8), step)
            to = pl.ds(pl.multiple_of(j * size + low * step, 8), step)
            pairs = ((proj.at[:, mine], whole[u].at[0:3, to]), (out.at[mine], whole[u].at[3, to]))
        else:
            step = units[u][0].shape[0] // GROUP
            pairs = ((units[u][0].at[pl.ds(pl.multiple_of(low * step, 8), step)], part(u, j, low, None)),)
        return [copy(src if sending else dst, dst, u, k - 1, (K_Z, K_Z2)[i], device) for i, (src, dst) in enumerate(pairs)]

    def z_send(u, k):
        for c in z_copies(u, k, z, (dp, (z + k) % nz), True):
            c.start()

    def source(k):
        return (z + nz - k) % nz

    def peer(u, k, kind, sending):
        if kind < K_C:
            sent, got, half, device = {
                K_X: (low, sl_x, None, dev_x),
                K_Y: (low, sl_y, None, dev_y),
                K_A: (sl_x, sl_d, 0, dev_y),
                K_B: (sl_y, sl_d, 1, dev_x),
            }[kind]
        else:
            sent, half = ((low, None), (sl_x, None), (sl_y, None), (sl_d, 0), (sl_d, 1))[kind - K_C]
            device = dev_c
            got = sent + 1 - 2 * core
        block = part(u, source(k), sent if sending else got, half)
        return copy(block, block, u, k - 1, kind, device)

    def stage1(u, k):
        for c in z_copies(u, k, source(k), dev_x, False):
            c.wait_recv()
        for kind in (K_X, K_Y, K_C):
            peer(u, k, kind, True).start()

    def stage2(u, k):
        peer(u, k, K_X, False).wait_recv()
        peer(u, k, K_A, True).start()
        peer(u, k, K_C + 1, True).start()
        peer(u, k, K_Y, False).wait_recv()
        peer(u, k, K_B, True).start()
        peer(u, k, K_C + 2, True).start()

    def stage3(u, k):
        peer(u, k, K_A, False).wait_recv()
        peer(u, k, K_C + 3, True).start()
        peer(u, k, K_B, False).wait_recv()
        peer(u, k, K_C + 4, True).start()

    sequence = [(u, k) for u in range(len(units)) for k in range(1, nz)]

    def step(n):
        if n < len(sequence):
            u, k = sequence[n]
            stage1(u, k)
            if u + 2 < len(units):
                z_send(u + 2, k)
        if 1 <= n < len(sequence) + 1:
            stage2(*sequence[n - 1])
        if 2 <= n < len(sequence) + 2:
            stage3(*sequence[n - 2])

    def arrived(u):
        for k in range(1, nz):
            for kind in range(K_C, K_C + 5):
                peer(u, k, kind, False).wait_recv()

    def sent(u):
        for k in range(1, nz):
            for c in z_copies(u, k, z, (dp, (z + k) % nz), True):
                c.wait_send()
            for kind in range(K_X, K_C + 5):
                peer(u, k, kind, True).wait_send()

    def loads(u, dst, sem):
        if is_attention(u):
            proj, out = units[u]
            size = out.shape[0]
            own = pl.ds(pl.multiple_of(z * size, 8), size)
            pairs = [(proj, dst.at[0:3, own]), (out, dst.at[3, own])]
            for k in range(1, nz):
                rows = pl.ds(pl.multiple_of(source(k) * size, 8), size)
                pairs.append((whole[u].at[:, rows], dst.at[:, rows]))
        else:
            pairs = [(units[u][0], dst.at[z])]
            for k in range(1, nz):
                pairs.append((whole[u].at[source(k)], dst.at[source(k)]))
        return [pltpu.make_async_copy(src, to, sem.at[i]) for i, (src, to) in enumerate(pairs)]

    return z_send, step, arrived, sent, loads


def project(x_ref, xrows, w_ref, w0, bias_ref, b0, out_ref):
    x = x_ref[xrows, :]
    tiles = D // TILE

    def body(i, carry):
        c, t = i // tiles, i % tiles
        at = pl.ds(pl.multiple_of(t * TILE, TILE), TILE)
        y = dot(x, w_ref[w0 + c, at, :], ((1,), (1,)))
        out_ref[c, xrows, at] = (y + bias_ref[pl.ds(b0 + c, 1), at]).astype(BF)
        return carry

    lax.fori_loop(0, 3 * tiles, body, 0)


def half_lanes():
    lane = lax.broadcasted_iota(jnp.int32, (1, 2 * HEAD_DIM), 1)
    return lane < HEAD_DIM


def attend(qkv_ref, ctx_ref, p_ref, mask_ref, q0, lq, k0, lk):
    first = half_lanes()
    keep = [jnp.where(first, HEAD_DIM**-0.5, 0.0).astype(BF), jnp.where(first, 0.0, HEAD_DIM**-0.5).astype(BF)]

    def body(pair, carry):
        lanes = pl.ds(pl.multiple_of(pair * 2 * HEAD_DIM, 2 * HEAD_DIM), 2 * HEAD_DIM)
        for g in range(2):
            qr, kr = pl.ds(q0 + g * lq, lq), pl.ds(k0 + g * lk, lk)
            q, k, v = qkv_ref[0, qr, lanes], qkv_ref[1, kr, lanes], qkv_ref[2, kr, lanes]
            parts = []
            for h in range(2):
                s = dot(q * keep[h], k, ((1,), (1,))) + mask_ref[g]
                w = jnp.exp(s - jnp.max(s, axis=1, keepdims=True))
                pb = (w * (1.0 / jnp.sum(w, axis=1, keepdims=True))).astype(BF)
                p_ref[g, 2 * pair + h] = pb
                parts.append(dot(pb, v, ((1,), (0,))))
            ctx_ref[qr, lanes] = jnp.where(first, parts[0], parts[1]).astype(BF)
        return carry

    lax.fori_loop(0, D // (2 * HEAD_DIM), body, 0, unroll=2)


def out_norm(ctx_ref, start, count, w_ref, wi, resid_ref, vec_ref, v0, pre_ref, hat_ref, rstd_ref, full_ref, low_ref):
    rows = pl.ds(start, count)
    ctx = ctx_ref[rows, :]

    def tile(t, carry):
        at = pl.ds(pl.multiple_of(t * TILE, TILE), TILE)
        y = dot(ctx, w_ref[wi, :, at], ((1,), (0,)))
        pre_ref[rows, at] = y + resid_ref[rows, at].astype(F32) + vec_ref[pl.ds(v0, 1), at]
        return carry

    lax.fori_loop(0, D // TILE, tile, 0)
    gain, shift = vec_ref[v0 + 1 : v0 + 2, :], vec_ref[v0 + 2 : v0 + 3, :]

    def norm(i, carry):
        r = pl.ds(pl.multiple_of(start + i * 32, 16), 32)
        x = pre_ref[r, :]
        center = x - jnp.sum(x, axis=1, keepdims=True) * (1.0 / D)
        rstd = lax.rsqrt(jnp.sum(center * center, axis=1, keepdims=True) * (1.0 / D) + LAYER_EPS)
        hat = center * rstd
        y = hat * gain + shift
        hat_ref[r, :] = hat.astype(BF)
        rstd_ref[r, :] = jnp.broadcast_to(rstd, (32, 128))
        full_ref[r, :] = y
        low_ref[r, :] = y.astype(BF)
        return carry

    lax.fori_loop(0, count // 32, norm, 0)


def by_group(src_ref, dst_ref, start, slots):
    half = slots * GROUP // 2
    low = lax.broadcasted_iota(jnp.int32, (8, D), 0) < 4

    def body(i, carry):
        a = [src_ref[4 * i + t].astype(F32) for t in range(4)]
        for g in range(2):
            rows = []
            for t in (0, 2):
                one, two = (a[t], pltpu.roll(a[t + 1], 4, 0)) if g == 0 else (pltpu.roll(a[t], 4, 0), a[t + 1])
                rows.append(jnp.where(low, one, two))
            at = pl.ds(pl.multiple_of(start + g * half + 16 * i, 16), 16)
            dst_ref[at, :] = jnp.concatenate(rows, axis=0).astype(dst_ref.dtype)
        return carry

    lax.fori_loop(0, slots // 4, body, 0)


def fill_masks(mask_refs, counts, first):
    for n, (ref, count) in enumerate(zip(mask_refs, counts)):
        for g in range(2):
            shape = ref.shape[1:]
            row, col = (lax.broadcasted_iota(jnp.int32, shape, d) for d in range(2))
            item = jnp.bitwise_and(col, 3)
            limit = jnp.zeros(shape, jnp.int32)
            for j in range(4):
                limit = jnp.where(item == j, count[first + 4 * g + j], limit)
            seen = jnp.logical_and(jnp.bitwise_and(row, 3) == item, jnp.right_shift(col, 2) < limit)
            ref[g] = jnp.where(seen, 0.0, MASKED).astype(F32)


SLOTS = 4
PARTS = 3


def scatter_steps(nz, mixed, slot_bufs, send_sem, recv_sem, rs_out):
    grad, crecv, xa, yb, ya, xb, zbuf, zrecv = slot_bufs
    dp, z, core, bx, by = place()
    dev_c = (dp + 1 - 2 * core, z)
    dev_x = (dp + 2 - 4 * bx, z)
    dev_y = (dp + 4 - 8 * by, z)
    rows, width = crecv.shape[3], crecv.shape[4]
    half = width // 2
    lo, hi = pl.ds(0, half), pl.ds(half, half)
    zw = width // nz
    S_C, S_XA, S_YB, S_YA, S_XB, S_Z = 0, 1, 2, 3, 4, 5

    def part(i, y, x, c, lanes):
        return grad.at[(i // PARTS) % 2, y, x, c, pl.ds((i % PARTS) * rows, rows), lanes]

    def remote(src, dst, s, k, device):
        return pltpu.make_async_remote_copy(
            src_ref=src, dst_ref=dst, send_sem=send_sem.at[s, k], recv_sem=recv_sem.at[s, k], device_id=device, device_id_type=MESH
        )

    every = slice(None)

    def core_copy(i):
        s = i % SLOTS
        return remote(part(i, every, every, 1 - core, every), crecv.at[s], s, S_C, dev_c)

    def xa_copy(i):
        s = i % SLOTS
        return remote(part(i, every, 1 - bx, core, lo), xa.at[s], s, S_XA, dev_x)

    def yb_copy(i):
        s = i % SLOTS
        return remote(part(i, 1 - by, every, core, hi), yb.at[s], s, S_YB, dev_y)

    def ya_copy(i):
        s = i % SLOTS
        return remote(part(i, 1 - by, bx, core, lo), ya.at[s], s, S_YA, dev_y)

    def xb_copy(i):
        s = i % SLOTS
        return remote(part(i, by, 1 - bx, core, hi), xb.at[s], s, S_XB, dev_x)

    def z_copy(s, k):
        return remote(zbuf.at[s, (z + k) % nz], zrecv.at[s, k - 1], s, S_Z + k - 1, (dp, (z + k) % nz))

    def merge(dst, src):
        for r in range(0, rows, 16):
            at = pl.ds(r, 16)
            dst[at] = dst[at] + src[at]

    def stage_a(i):
        s = i % SLOTS
        core_copy(i).wait()

        def body(j, carry):
            merge(part(i, j // 2, j % 2, core, every), crecv.at[s, j // 2, j % 2])
            return carry

        lax.fori_loop(0, 4, body, 0)
        xa_copy(i).start()
        yb_copy(i).start()

    def stage_b(i):
        s = i % SLOTS
        xa_copy(i).wait()
        yb_copy(i).wait()

        def body(j, carry):
            merge(part(i, j, bx, core, lo), xa.at[s, j])
            merge(part(i, by, j, core, hi), yb.at[s, j])
            return carry

        lax.fori_loop(0, 2, body, 0)
        ya_copy(i).start()
        xb_copy(i).start()

    def stage_c(i):
        s = i % SLOTS
        ya_copy(i).wait()
        xb_copy(i).wait()
        own = part(i, by, bx, core, every)
        for r in range(0, rows, 16):
            at = pl.ds(r, 16)
            left = own[at, lo] + ya[s, at, :]
            right = own[at, hi] + xb[s, at, :]
            full = jnp.concatenate([left, right], axis=1)
            for t in range(nz):
                if mixed[i // PARTS]:
                    sub = zw // 4
                    row = [full[:, m * (width // 4) + t * sub : m * (width // 4) + (t + 1) * sub] for m in range(4)]
                    zbuf[s, t, at, :] = jnp.concatenate(row, axis=1)
                else:
                    zbuf[s, t, at, :] = full[:, t * zw : (t + 1) * zw]
        for k in range(1, nz):
            z_copy(s, k).start()

    def stage_d(i):
        s = i % SLOTS
        for k in range(1, nz):
            z_copy(s, k).wait()
        for r in range(0, rows, 16):
            at = pl.ds(r, 16)
            total = zbuf[s, z, at, :].astype(F32)
            for k in range(nz - 1):
                total = total + zrecv[s, k, at, :].astype(F32)
            rs_out[i, at, :] = total

    return core_copy, stage_a, stage_b, stage_c, stage_d


def small_steps(nz, small, sbuf, srecv, szrecv, small_out, send_sem, recv_sem):
    dp, z, core, bx, by = place()
    devs = ((dp + 1 - 2 * core, z), (dp + 2 - 4 * bx, z), (dp + 4 - 8 * by, z))

    def remote(src, dst, k, device):
        return pltpu.make_async_remote_copy(
            src_ref=src, dst_ref=dst, send_sem=send_sem.at[k], recv_sem=recv_sem.at[k], device_id=device, device_id_type=MESH
        )

    def pair(k):
        return remote(sbuf.at[k], srecv.at[k], k, devs[k])

    def along_z(k, sending):
        return remote(sbuf.at[3], szrecv.at[z if sending else (z + nz - k) % nz], 2 + k, (dp, (z + k) % nz))

    def stage(k):
        if k == 0:
            sbuf[0] = small[...]
            pair(0).start()
        elif k < 4:
            pair(k - 1).wait()
            sbuf[k] = sbuf[k - 1] + srecv[k - 1]
            if k < 3:
                pair(k).start()
            else:
                szrecv[z] = sbuf[3]
                for i in range(1, nz):
                    along_z(i, True).start()
        else:
            for i in range(1, nz):
                along_z(i, True).wait_send()
                along_z(i, False).wait_recv()
            total = szrecv[0]
            for i in range(1, nz):
                total = total + szrecv[i]
            small_out[...] = total

    return stage


def eighth(x):
    return jnp.sum(x.reshape(x.shape[0] // 8, 8, x.shape[1]), axis=0)


def transpose_into(t_ref, x_ref, start, count):
    for i in range(D // 128):
        t_ref[i * 128 : (i + 1) * 128, 0:count] = x_ref[pl.ds(start, count), i * 128 : (i + 1) * 128].T


def feed_forward(nb_ref, rows, w_ref, bias_ref, b0, h_ref, slope_ref, first, last):
    x = nb_ref[rows, :]
    tiles = D // TILE

    def body(i, carry):
        zb, t = i // tiles, i % tiles
        at = pl.ds(pl.multiple_of(t * TILE, TILE), TILE)
        u = dot(x, w_ref[zb, :, at], ((1,), (0,))) + bias_ref[pl.ds(b0 + zb, 1), at]
        phi = 0.5 + 0.5 * lax.erf(u * 0.5**0.5)
        h_ref[zb, rows, at] = (u * phi).astype(BF)
        slope_ref[zb, rows, at] = (phi + u * (jnp.exp(-0.5 * u * u) * 0.3989422804014327)).astype(BF)
        return carry

    lax.fori_loop(first * tiles, last * tiles, body, 0)


def feed_out_rows(h_ref, rows, w_ref, nn_ref, vec_ref, v0, res_ref):
    def body(t, carry):
        at = pl.ds(pl.multiple_of(t * TILE, TILE), TILE)
        y = nn_ref[rows, at] + vec_ref[pl.ds(v0, 1), at]
        for zb in range(h_ref.shape[0]):
            y = y + dot(h_ref[zb, rows, :], w_ref[zb, :, at], ((1,), (0,)))
        res_ref[rows, at] = y
        return carry

    lax.fori_loop(0, D // TILE, body, 0)


def norm_grad(hat, rstd, gain, g, acc):
    scaled = g * gain
    dz = rstd * (
        scaled - jnp.sum(scaled, axis=1, keepdims=True) * (1.0 / D) - hat * (jnp.sum(scaled * hat, axis=1, keepdims=True) * (1.0 / D))
    )
    return dz, (acc[0] + eighth(dz), acc[1] + eighth(g * hat), acc[2] + eighth(g))


def no_sums():
    return tuple(jnp.zeros((8, D), F32) for _ in range(3))


def keep_sums(acc, small, row):
    for i in range(3):
        small[row + i : row + i + 1, :] = jnp.sum(acc[i], axis=0, keepdims=True)


def last_norm(start, count, res_ref, vec_ref, v0, cot_ref, weight_ref, result_ref, db_ref, small, row):
    gain, shift = vec_ref[v0 + 1 : v0 + 2, :], vec_ref[v0 + 2 : v0 + 3, :]

    def body(i, acc):
        r = pl.ds(pl.multiple_of(start + i * 32, 16), 32)
        x = res_ref[r, :]
        center = x - jnp.sum(x, axis=1, keepdims=True) * (1.0 / D)
        rstd = lax.rsqrt(jnp.sum(center * center, axis=1, keepdims=True) * (1.0 / D) + LAYER_EPS)
        hat = center * rstd
        result_ref[r, :] = (hat * gain + shift).astype(BF)
        g = cot_ref[r, :].astype(F32) * weight_ref[r, 0:1]
        dz, acc = norm_grad(hat, rstd, gain, g, acc)
        res_ref[r, :] = dz
        db_ref[r, :] = dz.astype(BF)
        return acc

    keep_sums(lax.fori_loop(0, count // 32, body, no_sums()), small, row)


def norm_back(start, count, res_ref, hat_ref, rstd_ref, vec_ref, gain_row, db_ref, small, row):
    gain = vec_ref[gain_row : gain_row + 1, :]

    def body(i, acc):
        r = pl.ds(pl.multiple_of(start + i * 32, 16), 32)
        dz, acc = norm_grad(hat_ref[r, :].astype(F32), rstd_ref[r, 0:1], gain, res_ref[r, :], acc)
        res_ref[r, :] = dz
        db_ref[r, :] = dz.astype(BF)
        return acc

    keep_sums(lax.fori_loop(0, count // 32, body, no_sums()), small, row)


def hidden_grad(db_ref, rows, w_ref, slope_ref, small, row):
    db = db_ref[rows, :]
    tiles = D // TILE

    def body(i, carry):
        zb, t = i // tiles, i % tiles
        at = pl.ds(pl.multiple_of(t * TILE, TILE), TILE)
        du = (dot(db, w_ref[zb, at, :], ((1,), (1,))) * slope_ref[zb, rows, at].astype(F32)).astype(BF)
        slope_ref[zb, rows, at] = du
        small[pl.ds(row + zb, 1), at] = jnp.sum(eighth(du.astype(F32)), axis=0, keepdims=True)
        return carry

    lax.fori_loop(0, slope_ref.shape[0] * tiles, body, 0)


def add_products(res_ref, out_ref, rows, x_ref, count, w_ref, transposed):
    def body(t, carry):
        at = pl.ds(pl.multiple_of(t * TILE, TILE), TILE)
        y = res_ref[rows, at]
        for c in range(count):
            if transposed:
                y = y + dot(x_ref[c, rows, :], w_ref[c, at, :], ((1,), (1,)))
            else:
                y = y + dot(x_ref[c, rows, :], w_ref[c, :, at], ((1,), (0,)))
        out_ref[rows, at] = y
        return carry

    lax.fori_loop(0, D // TILE, body, 0)


def context_grad(db_ref, rows, w_ref, dctx_ref):
    db = db_ref[rows, :]

    def body(t, carry):
        at = pl.ds(pl.multiple_of(t * TILE, TILE), TILE)
        dctx_ref[rows, at] = dot(db, w_ref[3, at, :], ((1,), (1,))).astype(BF)
        return carry

    lax.fori_loop(0, D // TILE, body, 0)


def attend_back(qkv_ref, dctx_ref, p_ref, out_ref, q0, lq, k0, lk, first_pair=0, last_pair=D // (2 * HEAD_DIM)):
    first = half_lanes()
    keep = [jnp.where(first, 1.0, 0.0).astype(BF), jnp.where(first, 0.0, 1.0).astype(BF)]

    def body(pair, carry):
        lanes = pl.ds(pl.multiple_of(pair * 2 * HEAD_DIM, 2 * HEAD_DIM), 2 * HEAD_DIM)
        for g in range(2):
            qr, kr = pl.ds(q0 + g * lq, lq), pl.ds(k0 + g * lk, lk)
            q, k, v, dc = qkv_ref[0, qr, lanes], qkv_ref[1, kr, lanes], qkv_ref[2, kr, lanes], dctx_ref[qr, lanes]
            dq, dk, dv = [], [], []
            for h in range(2):
                pb = p_ref[g, 2 * pair + h]
                p = pb.astype(F32)
                dp = dot(dc * keep[h], v, ((1,), (1,)))
                ds = (p * (dp - jnp.sum(p * dp, axis=1, keepdims=True))).astype(BF)
                dq.append(dot(ds, k, ((1,), (0,))))
                dk.append(dot(ds, q, ((0,), (0,))))
                dv.append(dot(pb, dc, ((0,), (0,))))
            out_ref[0, qr, lanes] = (jnp.where(first, dq[0], dq[1]) * HEAD_DIM**-0.5).astype(BF)
            out_ref[1, kr, lanes] = (jnp.where(first, dk[0], dk[1]) * HEAD_DIM**-0.5).astype(BF)
            out_ref[2, kr, lanes] = jnp.where(first, dv[0], dv[1]).astype(BF)
        return carry

    lax.fori_loop(first_pair, last_pair, body, 0)


def bias_sums(x_ref, rows, count, small, row_q, row_v, add):
    ones = jnp.ones((8, count), BF)
    for c, row in ((0, row_q), (2, row_v)):
        total = dot(ones, x_ref[c, rows, :], ((1,), (0,)))[0:1, :]
        small[row : row + 1, :] = total


def grad_tiles(grad_ref, m, t_ref, count, x_ref, rows, first, last, lane0, mats):
    size = grad_ref.shape[4]
    left = t_ref[:, 0:count]
    tiles = D // TILE

    def body(i, carry):
        b, t = i // tiles, i % tiles
        at = pl.ds(pl.multiple_of(t * TILE, TILE), TILE)
        right = x_ref[b, rows, at] if mats else x_ref[rows, at]
        y = dot(left, right, ((1,), (0,))).astype(BF)
        lanes = pl.ds(pl.multiple_of(lane0 + i * TILE, TILE), TILE)
        grad_ref[m % 2, :, :, :, :, lanes] = y.reshape(2, 2, 2, size, TILE)
        return carry

    lax.fori_loop(first * tiles, last * tiles, body, 0)


CROSS, SELF1, IN1, OUT1, SELF0, IN0, OUT0 = range(7)
MIXED = (False, False, True, False, False, True, True)


def layer_kernel(nz, lens, *refs):
    cp, co, sp, so, fi, fo, word_count, region_count, flags = refs[:9]
    lang, vis, cot_lang, cot_vis, cross_b, self_b, feed_b = refs[9:16]
    cob, cg, cs, sob, sg, ss, fob, fg, fs = refs[16:25]
    whole = refs[25:32]
    rs_out, small_out, result, res = refs[32:36]
    wb0, wb1, wb2, x, qkv_c, ctx_c, p_c0, p_c1, hat1, rstd1, mb = refs[36:47]
    qkv_s, ctx_s, p_s0, p_s1, hat2, rstd2, mid, nb, hid, slope, db, dctx, t1, t2, small = refs[47:62]
    grad, crecv, xa, yb, ya, xb, zbuf, zrecv, sbuf, srecv, szrecv = refs[62:73]
    bias_src, bias_all, bias_ref, vec, weight = refs[73:78]
    masks = refs[78:82]
    send_sem, recv_sem, w_sem, bias_send, bias_recv, rs_send, rs_recv, small_send, small_recv = refs[82:]
    dp, z, core, bx, by = place()
    lw, lv = lens
    rw, rv = 2 * lw, 2 * lv
    start, count = (0, rw), (rw, rv)
    rows = (pl.ds(0, rw), pl.ds(rw, rv))
    every = pl.ds(0, rw + rv)

    bias_src[...] = jnp.zeros_like(bias_src)
    part = cross_b.shape[1]
    for t in range(nz):

        @pl.when(z == t)
        def _(t=t):
            lanes = slice(t * part, (t + 1) * part)
            for i in range(2):
                bias_src[2 * i : 2 * i + 1, lanes] = cross_b[i : i + 1, :]
                for s in range(2):
                    bias_src[3 + 3 * s + 2 * i : 4 + 3 * s + 2 * i, lanes] = self_b[s, i : i + 1, :]
            for s in range(2):
                bias_src[9 + nz * s + t : 10 + nz * s + t, :] = feed_b[s : s + 1, :]

    targets = [((dp + 1 - 2 * core, z), None), ((dp + 2 - 4 * bx, z), None), ((dp + 4 - 8 * by, z), None)]
    for k in range(1, nz):
        targets.append(((dp, (z + k) % nz), None))
    greet(targets)
    units = (
        (cp, co),
        (sp.at[1], so.at[1]),
        (fi.at[1],),
        (fo.at[1],),
        (sp.at[0], so.at[0]),
        (fi.at[0],),
        (fo.at[0],),
    )
    z_send, gather, arrived, sent, loads = gather_steps(nz, units, whole, send_sem, recv_sem)
    slot_bufs = (grad, crecv, xa, yb, ya, xb, zbuf, zrecv)
    core_copy, stage_a, stage_b, stage_c, stage_d = scatter_steps(nz, MIXED, slot_bufs, rs_send, rs_recv, rs_out)
    small_stage = small_steps(nz, small, sbuf, srecv, szrecv, small_out, small_send, small_recv)
    pieces = len(MIXED) * PARTS

    def scatter(n):
        if n + 1 < pieces:
            core_copy(n + 1).start()
        if n < pieces:
            stage_a(n)
        if 1 <= n < pieces + 1:
            stage_b(n - 1)
        if 2 <= n < pieces + 2:
            stage_c(n - 2)
        if n >= 3:
            stage_d(n - 3)

    def bias_copy(k, sending):
        return pltpu.make_async_remote_copy(
            src_ref=bias_src,
            dst_ref=bias_all.at[z if sending else (z + nz - k) % nz],
            send_sem=bias_send.at[k],
            recv_sem=bias_recv.at[k],
            device_id=(dp, (z + k) % nz),
            device_id_type=MESH,
        )

    def fetch(u, dst, turn=0, wait=True):
        if turn == 0:
            arrived(u)
        for c in loads(u, dst, w_sem.at[u + turn]):
            c.start()

    def ready(u, dst, turn=0):
        for c in loads(u, dst, w_sem.at[u + turn]):
            c.wait()

    cot = dctx

    def prepare():
        for i, ref in enumerate((cob, cg, cs)):
            vec[i : i + 1, :] = ref[...].reshape(1, D)
        for s in range(2):
            for i, ref in enumerate((sob, sg, ss)):
                vec[3 + 3 * s + i : 4 + 3 * s + i, :] = ref[s : s + 1, :]
            for i, ref in enumerate((fob, fg, fs)):
                vec[9 + 3 * s + i : 10 + 3 * s + i, :] = ref[s : s + 1, :]
        by_group(lang, x, 0, lang.shape[0])
        by_group(vis, x, rw, vis.shape[0])
        by_group(cot_lang, cot, 0, cot_lang.shape[0])
        by_group(cot_vis, cot, rw, cot_vis.shape[0])
        fill_masks(masks, (region_count, word_count, word_count, region_count), z * GROUP)
        for s in range(2):
            for g in range(2):
                row = lax.broadcasted_iota(jnp.int32, (lens[s], 128), 0)
                item = jnp.bitwise_and(row, 3)
                value = jnp.zeros((lens[s], 128), F32)
                for j in range(4):
                    n = 4 * g + j
                    other = flags[0, n].astype(F32)
                    if s == 0:
                        answer = jnp.maximum(flags[1, n], flags[2, n]).astype(F32)
                        value = jnp.where(item == j, jnp.where(row < 4, answer, other), value)
                    else:
                        value = jnp.where(item == j, other, value)
                weight[start[s] + g * lens[s] : start[s] + (g + 1) * lens[s], :] = value

    def bias_sum():
        for k in range(1, nz):
            bias_copy(k, False).wait_recv()
        bias_all[z] = bias_src[...]
        total = bias_all[0]
        for k in range(1, nz):
            total = total + bias_all[k]
        bias_ref[...] = total

    w_self, w_in, w_out = (wb0, wb1), (wb2, wb2), (wb1, wb0)
    u_self, u_in, u_out = (SELF0, SELF1), (IN0, IN1), (OUT0, OUT1)

    def cross_project_all():
        ready(CROSS, wb0)
        bias_sum()
        project(x, every, wb0, 0, bias_ref, 0, qkv_c)

    def cross_forward(s):
        if s == 0:
            attend(qkv_c, ctx_c, p_c0, masks[0], 0, lw, rw, lv)
        else:
            attend(qkv_c, ctx_c, p_c1, masks[1], rw, lv, 0, lw)

    def cross_norm(s):
        out_norm(ctx_c, start[s], count[s], wb0, 3, x, vec, 0, res, hat1, rstd1, mid, mb)

    def self_project(s):
        ready(u_self[s], w_self[s])
        project(mb, rows[s], w_self[s], 0, bias_ref, 3 + 3 * s, qkv_s)

    def self_forward(s):
        attend(qkv_s, ctx_s, (p_s0, p_s1)[s], masks[2 + s], start[s], lens[s], start[s], lens[s])

    def self_norm(s):
        out_norm(ctx_s, start[s], count[s], w_self[s], 3, mid, vec, 3 + 3 * s, res, hat2, rstd2, mid, nb)

    def forward(s, first, last):
        if first == 0:
            ready(u_in[s], w_in[s])
        feed_forward(nb, rows[s], w_in[s], bias_ref, 9 + nz * s, hid, slope, first, last)

    def out_rows(s):
        ready(u_out[s], w_out[s])
        feed_out_rows(hid, rows[s], w_out[s], mid, vec, 9 + 3 * s, res)

    def norm3(s):
        last_norm(start[s], count[s], res, vec, 9 + 3 * s, cot, weight, result, db, small, 15 + 3 * s)

    def du(s):
        hidden_grad(db, rows[s], w_out[s], slope, small, 21 + nz * s)

    def dn(s):
        add_products(res, res, rows[s], slope, nz, w_in[s], True)

    def self_in(s):
        norm_back(start[s], count[s], res, hat2, rstd2, vec, 4 + 3 * s, db, small, 7 + 5 * s)
        context_grad(db, rows[s], w_self[s], dctx)

    def self_back(s, first, last):
        attend_back(qkv_s, dctx, (p_s0, p_s1)[s], hid, start[s], lens[s], start[s], lens[s], first, last)

    def self_sums(s):
        bias_sums(hid, rows[s], count[s], small, 5 + 5 * s, 6 + 5 * s, False)

    def dm(s):
        add_products(res, res, rows[s], hid, 3, w_self[s], False)

    def cross_in():
        ready(CROSS, wb1, 7)
        norm_back(0, rw + rv, res, hat1, rstd1, vec, 1, nb, small, 2)
        context_grad(nb, every, wb1, dctx)

    def cross_back(s):
        attend_back(qkv_c, dctx, (p_c0, p_c1)[s], slope, start[s], lens[s], start[1 - s], lens[1 - s])

    def cross_sums():
        bias_sums(slope, every, rw + rv, small, 0, 1, False)
        small_stage(0)

    def finish_rows():
        add_products(res, res, every, slope, 3, wb1, False)

    def grads(m):
        if m < 6:
            s = 1 - m // 3
            if m % 3 < 2:
                turned, src, right = ((t1, db, hid), (t2, nb, slope))[m % 3]
                transpose_into(turned, src, start[s], count[s])
                grad_tiles(grad, m, turned, count[s], right, rows[s], 0, nz, 0, True)
                return
            src, at, n, back, ctx, dqkv, dz = mb, start[s], count[s], rows[s], ctx_s, hid, db
        else:
            src, at, n, back, ctx, dqkv, dz = x, 0, rw + rv, every, ctx_c, slope, nb
        transpose_into(t1, dz, at, n)
        transpose_into(t2, src, at, n)
        grad_tiles(grad, m, t2, n, dqkv, back, 0, 3, 0, True)
        grad_tiles(grad, m, t1, n, ctx, back, 0, 1, 3 * D, False)

    for k in range(1, nz):
        z_send(0, k)
    for k in range(1, nz):
        bias_copy(k, True).start()
    for k in range(1, nz):
        z_send(1, k)
    prepare()
    for n in range(5):
        gather(n)
    fetch(CROSS, wb0)
    gather(5)
    cross_project_all()
    gather(6)
    cross_forward(1)
    gather(7)
    fetch(SELF1, wb1)
    cross_norm(1)
    gather(8)
    self_project(1)
    gather(9)
    self_forward(1)
    gather(10)
    fetch(IN1, wb2)
    self_norm(1)
    cross_forward(0)
    gather(11)
    forward(1, 0, 2)
    cross_norm(0)
    gather(12)
    forward(1, 2, nz)
    gather(13)
    fetch(OUT1, wb0)
    out_rows(1)
    norm3(1)
    gather(14)
    grads(0)
    core_copy(0).start()
    du(1)
    scatter(0)
    gather(15)
    grads(1)
    scatter(1)
    gather(16)
    fetch(SELF0, wb0)
    dn(1)
    self_in(1)
    scatter(2)
    gather(17)
    self_back(1, 0, 3)
    scatter(3)
    gather(18)
    self_back(1, 3, 6)
    scatter(4)
    gather(19)
    fetch(IN0, wb2)
    dm(1)
    self_sums(1)
    grads(2)
    scatter(5)
    gather(20)
    self_project(0)
    self_forward(0)
    scatter(6)
    gather(21)
    self_norm(0)
    forward(0, 0, nz)
    scatter(7)
    gather(22)
    fetch(OUT0, wb1)
    out_rows(0)
    norm3(0)
    grads(3)
    scatter(8)
    du(0)
    fetch(CROSS, wb1, 7)
    scatter(9)
    dn(0)
    scatter(10)
    grads(4)
    scatter(11)
    self_in(0)
    self_back(0, 0, 6)
    scatter(12)
    dm(0)
    cross_in()
    scatter(13)
    self_sums(0)
    grads(5)
    scatter(14)
    cross_back(0)
    scatter(15)
    cross_back(1)
    scatter(16)
    grads(6)
    scatter(17)
    cross_sums()
    scatter(18)
    small_stage(1)
    finish_rows()
    scatter(19)
    small_stage(2)
    scatter(20)
    small_stage(3)
    scatter(21)
    small_stage(4)
    scatter(22)
    scatter(23)
    for u in range(len(units)):
        sent(u)
    for k in range(1, nz):
        bias_copy(k, True).wait_send()


def layer(nz, lens, shards, counts, flags, inputs, biases, vectors):
    rows = 2 * sum(lens)
    lw, lv = lens
    nh = D // HEAD_DIM
    size = D // GROUP // PARTS
    width = 4 * D
    any_spec = pl.BlockSpec(memory_space=pl.ANY)
    vmem = pl.BlockSpec(memory_space=pltpu.VMEM)
    smem = pl.BlockSpec(memory_space=pltpu.SMEM)
    sd = jax.ShapeDtypeStruct
    vm = pltpu.VMEM
    total = len(MIXED) * PARTS
    dma = pltpu.SemaphoreType.DMA
    act = vm((rows, D), BF)
    outs = pl.pallas_call(
        functools.partial(layer_kernel, nz, lens),
        out_shape=[sd((4, D, D), BF)] * 7
        + [sd((total, size, width // nz), F32), sd((32, D), F32), sd((rows, D), BF), sd((rows, D), F32)],
        in_specs=[any_spec] * 6 + [smem] * 3 + [vmem] * 16,
        out_specs=[any_spec] * 7 + [vmem] * 4,
        scratch_shapes=[
            vm((4, D, D), BF),
            vm((4, D, D), BF),
            vm((4, D, D), BF),
            act,
            vm((3, rows, D), BF),
            act,
            vm((2, nh, lw, lv), BF),
            vm((2, nh, lv, lw), BF),
            act,
            vm((rows, 128), F32),
            act,
            vm((3, rows, D), BF),
            act,
            vm((2, nh, lw, lw), BF),
            vm((2, nh, lv, lv), BF),
            act,
            vm((rows, 128), F32),
            vm((rows, D), F32),
            act,
            vm((nz, rows, D), BF),
            vm((nz, rows, D), BF),
            act,
            act,
            vm((D, rows), BF),
            vm((D, rows), BF),
            vm((32, D), F32),
            vm((2, 2, 2, 2, size * PARTS, width), BF),
            vm((SLOTS, 2, 2, size, width), BF),
            vm((SLOTS, 2, size, width // 2), BF),
            vm((SLOTS, 2, size, width // 2), BF),
            vm((SLOTS, size, width // 2), BF),
            vm((SLOTS, size, width // 2), BF),
            vm((SLOTS, nz, size, width // nz), BF),
            vm((SLOTS, nz - 1, size, width // nz), BF),
            vm((4, 32, D), F32),
            vm((3, 32, D), F32),
            vm((nz, 32, D), F32),
            vm((24, D), F32),
            vm((nz, 24, D), F32),
            vm((24, D), F32),
            vm((16, D), F32),
            vm((rows, 128), F32),
            vm((2, lw, lv), F32),
            vm((2, lv, lw), F32),
            vm((2, lw, lw), F32),
            vm((2, lv, lv), F32),
            dma((7, nz - 1, K_Z2 + 1)),
            dma((7, nz - 1, K_Z2 + 1)),
            dma((8, nz + 1)),
            dma((nz,)),
            dma((nz,)),
            dma((SLOTS, 4 + nz)),
            dma((SLOTS, 4 + nz)),
            dma((2 + nz,)),
            dma((2 + nz,)),
        ],
        compiler_params=pltpu.CompilerParams(collective_id=1, has_side_effects=True, vmem_limit_bytes=VMEM_BYTES),
        name="layer",
    )(*shards, *counts, flags, *inputs, *biases, *vectors)
    return outs[7:]


VMEM_BYTES = 62 << 20


def finish_kernel(es, nz, slots, *refs):
    loads = [pltpu.make_async_copy(src, dst, refs[30].at[i]) for i, (src, dst) in enumerate(zip(refs[:4], refs[26:30]))]
    for c in loads:
        c.start()
    sums, small, result, dinput = refs[26:30]
    refs = refs[:26]
    lang, vis, dlang, dvis, gcp, gcb, gco, gcob, gcg, gcs, gsp, gsb, gso, gsob, gsg, gss, gfi, gfib, gfo, gfob, gfg, gfs = refs[4:]
    parts, rows = sums.shape[1], sums.shape[2]
    low = lax.broadcasted_iota(jnp.int32, (8, D), 0) < 4

    def by_slot(src, dst, start, n):
        half = n * GROUP // 2

        def body(i, carry):
            g = [src[pl.ds(pl.multiple_of(start + h * half + 16 * i, 16), 16), :].astype(F32) for h in range(2)]
            for t in range(2):
                one, two = g[0][8 * t : 8 * t + 8], g[1][8 * t : 8 * t + 8]
                dst[4 * i + 2 * t] = jnp.where(low, one, pltpu.roll(two, 4, 0)).astype(dst.dtype)
                dst[4 * i + 2 * t + 1] = jnp.where(low, pltpu.roll(one, 4, 0), two).astype(dst.dtype)
            return carry

        lax.fori_loop(0, n // 4, body, 0)

    loads[2].wait()
    by_slot(result, lang, 0, slots[0])
    by_slot(result, vis, GROUP * slots[0], slots[1])
    loads[3].wait()
    by_slot(dinput, dlang, 0, slots[0])
    by_slot(dinput, dvis, GROUP * slots[0], slots[1])
    loads[0].wait()
    loads[1].wait()
    for s in range(2):
        first = 3 * (1 - s)
        for p in range(parts):
            gfo[s, p * rows : (p + 1) * rows, :] = sums[first, p]
            gfi[s, p * rows : (p + 1) * rows, :] = sums[first + 1, p]
    for i, proj, out in ((5, gsp.at[0], gso.at[0]), (2, gsp.at[1], gso.at[1]), (6, gcp, gco)):
        full = sums[i].reshape(parts * rows, D)
        for c in range(3):
            proj[c] = full[:, c * es : (c + 1) * es]
        out[...] = full[:, 3 * es :].T
    gcb[...] = small[0:2]
    for i, ref in enumerate((gcob, gcg, gcs)):
        ref[...] = small[2 + i : 3 + i].reshape(D)
    for s in range(2):
        gsb[s] = small[5 + 5 * s : 7 + 5 * s]
        for i, ref in enumerate((gsob, gsg, gss)):
            ref[s : s + 1] = small[7 + 5 * s + i : 8 + 5 * s + i]
        for i, ref in enumerate((gfob, gfg, gfs)):
            ref[s : s + 1] = small[15 + 3 * s + i : 16 + 3 * s + i]
        for t in range(nz):
            gfib[s : s + 1, t * D : (t + 1) * D] = small[21 + nz * s + t : 22 + nz * s + t]


def finish(es, nz, slots, sums, small, result, dinput):
    sd = jax.ShapeDtypeStruct
    chunk = D // GROUP
    vmem = pl.BlockSpec(memory_space=pltpu.VMEM)
    two, one = sd((2, D), F32), sd((D,), F32)
    shapes = (
        [sd((n, GROUP, D), dt) for dt in (BF, F32) for n in slots]
        + [sd((3, chunk, es), F32), two, sd((es, chunk), F32), one, one, one]
        + [sd((2, 3, chunk, es), F32), sd((2, 2, D), F32), sd((2, es, chunk), F32), two, two, two]
        + [sd((2, chunk, D), F32), sd((2, nz * D), F32), sd((2, chunk, D), F32), two, two, two]
    )
    return pl.pallas_call(
        functools.partial(finish_kernel, es, nz, slots),
        out_shape=shapes,
        in_specs=[pl.BlockSpec(memory_space=pltpu.HBM)] * 4,
        out_specs=[vmem] * len(shapes),
        scratch_shapes=[pltpu.VMEM(v.shape, v.dtype) for v in (sums, small, result, dinput)] + [pltpu.SemaphoreType.DMA((4,))],
        compiler_params=pltpu.CompilerParams(vmem_limit_bytes=40 << 20),
        name="finish",
    )(sums, small, result, dinput)


def dot(a, b, dims):
    return lax.dot_general(a, b, (dims, ((), ())), preferred_element_type=F32)


def per_device(nz, ndp, *args):
    (
        language,
        visual,
        word_count,
        region_count,
        task_flags,
        grad_language,
        grad_visual,
        cross_project,
        cross_bias,
        cross_out,
        cross_out_bias,
        cross_gain,
        cross_shift,
        self_project,
        self_bias,
        self_out,
        self_out_bias,
        self_gain,
        self_shift,
        feed_in,
        feed_in_bias,
        feed_out,
        feed_out_bias,
        feed_gain,
        feed_shift,
    ) = args
    items = language.shape[0]
    slots = (language.shape[1], visual.shape[1])
    counts_rows = (items * slots[0], items * slots[1])
    z = lax.axis_index("tensor")
    es = cross_project.shape[2]
    fs = feed_in.shape[2]
    lens = tuple(items // 2 * n for n in slots)
    shards = (jnp.swapaxes(cross_project, 1, 2), cross_out, jnp.swapaxes(self_project, 2, 3), self_out, feed_in, feed_out)
    sums, vectors, result, dinput = layer(
        nz,
        lens,
        shards,
        (word_count, region_count),
        task_flags.T,
        tuple(jnp.swapaxes(v, 0, 1) for v in (language, visual, grad_language, grad_visual)),
        (cross_bias, self_bias, feed_in_bias),
        (cross_out_bias, cross_gain, cross_shift, self_out_bias, self_gain, self_shift, feed_out_bias, feed_gain, feed_shift),
    )
    outer = ndp // GROUP
    if outer == 1:
        outs = list(finish(es, nz, slots, sums.reshape((7, PARTS) + sums.shape[1:]), vectors, result, dinput))
        for i in range(4):
            outs[i] = jnp.swapaxes(outs[i], 0, 1)
        outs[18] = jnp.swapaxes(outs[18], 1, 2)
        return tuple(outs)
    sums = sums.reshape(7, -1, sums.shape[2])
    if outer > 1:
        members = [[i * GROUP + j for i in range(outer)] for j in range(GROUP)]
        sums = lax.psum_scatter(sums, "dp", scatter_dimension=1, axis_index_groups=members, tiled=True)
        sums = lax.ppermute(sums, "dp", [(i * GROUP + j, j * outer + i) for i in range(outer) for j in range(GROUP)])
        vectors = lax.psum(vectors, "dp", axis_index_groups=members)
    names = [("out", 1), ("in", 1), ("self", 1), ("out", 0), ("in", 0), ("self", 0), "cross"]
    total = {name: sums[i] for i, name in enumerate(names)}

    def columns(v):
        return jnp.stack([v[:, i * es : (i + 1) * es] for i in range(3)]), v[:, 3 * es :].T

    gcp, gco = columns(total["cross"])
    gs = [columns(total["self", s]) for s in range(2)]
    v = vectors

    def by_item(x, s, shape):
        x = x[s * counts_rows[0] : s * counts_rows[0] + counts_rows[s]]
        return x.reshape(2, shape[1], shape[0] // 2, D).transpose(0, 2, 1, 3).reshape(shape)

    f0 = 21
    nf = nz * fs // D
    return (
        by_item(result, 0, language.shape),
        by_item(result, 1, visual.shape),
        by_item(dinput, 0, language.shape),
        by_item(dinput, 1, visual.shape),
        gcp,
        v[0:2],
        gco,
        v[2],
        v[3],
        v[4],
        jnp.stack([gs[0][0], gs[1][0]]),
        jnp.stack([v[5:7], v[10:12]]),
        jnp.stack([gs[0][1], gs[1][1]]),
        jnp.stack([v[7], v[12]]),
        jnp.stack([v[8], v[13]]),
        jnp.stack([v[9], v[14]]),
        jnp.stack([total["in", 0], total["in", 1]]),
        v[f0 : f0 + 2 * nf].reshape(2, nz * fs),
        jnp.stack([total["out", 0].T, total["out", 1].T]),
        jnp.stack([v[15], v[18]]),
        jnp.stack([v[16], v[19]]),
        jnp.stack([v[17], v[20]]),
    )


def solution(mesh):
    rows = P(("dp", "tensor"), None, None)
    placed = (
        rows,
        rows,
        P("dp"),
        P("dp"),
        P(("dp", "tensor"), None),
        rows,
        rows,
        P(None, None, "tensor"),
        P(None, "tensor"),
        P("tensor", None),
        P(),
        P(),
        P(),
        P(None, None, None, "tensor"),
        P(None, None, "tensor"),
        P(None, "tensor", None),
        P(),
        P(),
        P(),
        P(None, None, "tensor"),
        P(None, "tensor"),
        P(None, "tensor", None),
        P(),
        P(),
        P(),
    )
    return jax.shard_map(
        functools.partial(per_device, mesh.shape["tensor"], mesh.shape["dp"]),
        mesh=mesh,
        in_specs=placed,
        out_specs=(
            rows,
            rows,
            rows,
            rows,
            P(None, "dp", "tensor"),
            P(),
            P("tensor", "dp"),
            P(),
            P(),
            P(),
            P(None, None, "dp", "tensor"),
            P(),
            P(None, "tensor", "dp"),
            P(),
            P(),
            P(),
            P(None, "dp", "tensor"),
            P(),
            P(None, "tensor", "dp"),
            P(),
            P(),
            P(),
        ),
        check_vma=False,
    )
```

profile of v0, /device:TPU:0, one launch (start us, length us, event | category | flops | bytes accessed | tf_op | source)
XLA Modules:
  0.0 334.2 jit_solution(10448787705181300459)
XLA Ops:
  0.7 324.7 %layer.1 = (bf16[4,768,768]{2,1,0:T(8,128)(2,1)}, bf16[4,768,768]{2,1,0:T(8,128)(2,1)}, bf16[4,768,768]{2,1,0:T(8,128)(2,1)}, bf16[4,768,768]{2,1,0:T(8,128)(2,1...) custom-call(bf16[3,192,768]{2,1,0:T(8,128)(2,1)} %bitcast.15, ...), custom_call_target="tpu_custom_call" | custom-call | tf_op jit(solution)/shard_map/layer/pallas_call | solution.py:952
  325.4 0.0 copy-start
  325.4 1.6 copy-done
  327.0 0.0 copy-start.1
  327.0 1.3 copy-done.1
  328.3 0.0 copy-start.2
  328.3 1.1 copy-done.2
  329.4 0.0 copy-start.3
  329.4 0.9 copy-done.3
  330.3 3.7 %finish.1 = (bf16[20,8,768]{2,1,0:T(8,128)(2,1)}, bf16[36,8,768]{2,1,0:T(8,128)(2,1)}, f32[20,8,768]{2,1,0:T(8,128)}, f32[36,8,768]{2,1,0:T(8,128)}, f32[3,96,19...) custom-call(f32[7,3,32,768]{3,2,1,0:T(8,128)S(1)} %bitcast.13, ...), custom_call_target="tpu_custom_call" | custom-call | tf_op jit(solution)/shard_map/finish/pallas_call | solution.py:1089
Async XLA Ops:
  325.4 1.6 copy-start
  327.0 1.3 copy-start.1
  328.3 1.1 copy-start.2
  329.4 0.9 copy-start.3
where the time goes:
time: 334 us
  Pallas kernels  328 us (98%)
  local copies, waits for them, and re-layouts  4.9 us (1%)
    pallas_call x1, Pallas kernels, layer(): pl.pallas_call(functools.partial(layer_kernel, nz, lens), out_shape=[sd((...  325 us

commit v1 on v0

--- a/solution.py
+++ b/solution.py
@@ -43,11 +43,11 @@
     pl.semaphore_wait(barrier, count)
 
 
-K_Z, K_X, K_Y, K_A, K_B, K_C, K_Z2 = 0, 1, 2, 3, 4, 5, 10
+K_Z, K_X, K_Y, K_A, K_B, K_Z2, K_C = 0, 1, 2, 3, 4, 5, 6
 TILE = 256
 
 
-def gather_steps(nz, units, whole, send_sem, recv_sem):
+def gather_steps(nz, units, whole, send_sem, recv_sem, core_sem):
     dp, z, core, bx, by = place()
     low = dp % GROUP
     dev_c = (dp + 1 - 2 * core, z)
@@ -58,8 +58,9 @@
     sl_d = low + 2 - 4 * bx + 4 - 8 * by
 
     def copy(src, dst, u, k, kind, device):
+        got = core_sem.at[u] if kind >= K_C else recv_sem.at[u, k, kind]
         return pltpu.make_async_remote_copy(
-            src_ref=src, dst_ref=dst, send_sem=send_sem.at[u, k, kind], recv_sem=recv_sem.at[u, k, kind], device_id=device, device_id_type=MESH
+            src_ref=src, dst_ref=dst, send_sem=send_sem.at[u], recv_sem=got, device_id=device, device_id_type=MESH
         )
 
     def is_attention(u):
@@ -145,16 +146,12 @@
             stage3(*sequence[n - 2])
 
     def arrived(u):
-        for k in range(1, nz):
-            for kind in range(K_C, K_C + 5):
-                peer(u, k, kind, False).wait_recv()
+        block = whole[u].at[0 : nz - 1, 0 : D // 2]
+        pltpu.make_async_copy(block, block, core_sem.at[u]).wait()
 
     def sent(u):
-        for k in range(1, nz):
-            for c in z_copies(u, k, z, (dp, (z + k) % nz), True):
-                c.wait_send()
-            for kind in range(K_X, K_C + 5):
-                peer(u, k, kind, True).wait_send()
+        block = whole[u].at[0 : nz - 1]
+        pltpu.make_async_copy(block, block, send_sem.at[u]).wait()
 
     def loads(u, dst, sem):
         if is_attention(u):
@@ -276,6 +273,7 @@
 
 
 SLOTS = 4
+CORE_SLOTS = 7
 PARTS = 3
 
 
@@ -291,35 +289,32 @@
     zw = width // nz
     S_C, S_XA, S_YB, S_YA, S_XB, S_Z = 0, 1, 2, 3, 4, 5
 
-    def part(i, y, x, c, lanes):
-        return grad.at[(i // PARTS) % 2, y, x, c, pl.ds((i % PARTS) * rows, rows), lanes]
+    def part(i, c):
+        return grad.at[:, :, c, pl.ds((i % PARTS) * rows, rows)]
 
     def remote(src, dst, s, k, device):
         return pltpu.make_async_remote_copy(
             src_ref=src, dst_ref=dst, send_sem=send_sem.at[s, k], recv_sem=recv_sem.at[s, k], device_id=device, device_id_type=MESH
         )
 
-    every = slice(None)
-
     def core_copy(i):
-        s = i % SLOTS
-        return remote(part(i, every, every, 1 - core, every), crecv.at[s], s, S_C, dev_c)
+        return remote(part(i, 1 - core), crecv.at[i % CORE_SLOTS], i % CORE_SLOTS, S_C, dev_c)
 
     def xa_copy(i):
         s = i % SLOTS
-        return remote(part(i, every, 1 - bx, core, lo), xa.at[s], s, S_XA, dev_x)
+        return remote(crecv.at[i % CORE_SLOTS, :, 1 - bx, :, lo], xa.at[s], s, S_XA, dev_x)
 
     def yb_copy(i):
         s = i % SLOTS
-        return remote(part(i, 1 - by, every, core, hi), yb.at[s], s, S_YB, dev_y)
+        return remote(crecv.at[i % CORE_SLOTS, 1 - by, :, :, hi], yb.at[s], s, S_YB, dev_y)
 
     def ya_copy(i):
         s = i % SLOTS
-        return remote(part(i, 1 - by, bx, core, lo), ya.at[s], s, S_YA, dev_y)
+        return remote(crecv.at[i % CORE_SLOTS, 1 - by, bx, :, lo], ya.at[s], s, S_YA, dev_y)
 
     def xb_copy(i):
         s = i % SLOTS
-        return remote(part(i, by, 1 - bx, core, hi), xb.at[s], s, S_XB, dev_x)
+        return remote(crecv.at[i % CORE_SLOTS, by, 1 - bx, :, hi], xb.at[s], s, S_XB, dev_x)
 
     def z_copy(s, k):
         return remote(zbuf.at[s, (z + k) % nz], zrecv.at[s, k - 1], s, S_Z + k - 1, (dp, (z + k) % nz))
@@ -330,11 +325,11 @@
             dst[at] = dst[at] + src[at]
 
     def stage_a(i):
-        s = i % SLOTS
         core_copy(i).wait()
+        mine = part(i, core)
 
         def body(j, carry):
-            merge(part(i, j // 2, j % 2, core, every), crecv.at[s, j // 2, j % 2])
+            merge(crecv.at[i % CORE_SLOTS, j // 2, j % 2], mine.at[j // 2, j % 2])
             return carry
 
         lax.fori_loop(0, 4, body, 0)
@@ -347,8 +342,8 @@
         yb_copy(i).wait()
 
         def body(j, carry):
-            merge(part(i, j, bx, core, lo), xa.at[s, j])
-            merge(part(i, by, j, core, hi), yb.at[s, j])
+            merge(crecv.at[i % CORE_SLOTS, j, bx, :, lo], xa.at[s, j])
+            merge(crecv.at[i % CORE_SLOTS, by, j, :, hi], yb.at[s, j])
             return carry
 
         lax.fori_loop(0, 2, body, 0)
@@ -359,7 +354,7 @@
         s = i % SLOTS
         ya_copy(i).wait()
         xb_copy(i).wait()
-        own = part(i, by, bx, core, every)
+        own = crecv.at[i % CORE_SLOTS, by, bx]
         for r in range(0, rows, 16):
             at = pl.ds(r, 16)
             left = own[at, lo] + ya[s, at, :]
@@ -590,7 +585,7 @@
 
 
 def grad_tiles(grad_ref, m, t_ref, count, x_ref, rows, first, last, lane0, mats):
-    size = grad_ref.shape[4]
+    size = grad_ref.shape[3]
     left = t_ref[:, 0:count]
     tiles = D // TILE
 
@@ -600,7 +595,7 @@
         right = x_ref[b, rows, at] if mats else x_ref[rows, at]
         y = dot(left, right, ((1,), (0,))).astype(BF)
         lanes = pl.ds(pl.multiple_of(lane0 + i * TILE, TILE), TILE)
-        grad_ref[m % 2, :, :, :, :, lanes] = y.reshape(2, 2, 2, size, TILE)
+        grad_ref[:, :, :, :, lanes] = y.reshape(2, 2, 2, size, TILE)
         return carry
 
     lax.fori_loop(first * tiles, last * tiles, body, 0)
@@ -616,12 +611,14 @@
     cob, cg, cs, sob, sg, ss, fob, fg, fs = refs[16:25]
     whole = refs[25:32]
     rs_out, small_out, result, res = refs[32:36]
+    wb3 = refs[36]
+    refs = refs[1:]
     wb0, wb1, wb2, x, qkv_c, ctx_c, p_c0, p_c1, hat1, rstd1, mb = refs[36:47]
     qkv_s, ctx_s, p_s0, p_s1, hat2, rstd2, mid, nb, hid, slope, db, dctx, t1, t2, small = refs[47:62]
     grad, crecv, xa, yb, ya, xb, zbuf, zrecv, sbuf, srecv, szrecv = refs[62:73]
     bias_src, bias_all, bias_ref, vec, weight = refs[73:78]
     masks = refs[78:82]
-    send_sem, recv_sem, w_sem, bias_send, bias_recv, rs_send, rs_recv, small_send, small_recv = refs[82:]
+    send_sem, recv_sem, core_sem, w_sem, bias_send, bias_recv, rs_send, rs_recv, small_send, small_recv = refs[82:]
     dp, z, core, bx, by = place()
     lw, lv = lens
     rw, rv = 2 * lw, 2 * lv
@@ -656,14 +653,14 @@
         (fi.at[0],),
         (fo.at[0],),
     )
-    z_send, gather, arrived, sent, loads = gather_steps(nz, units, whole, send_sem, recv_sem)
+    z_send, gather, arrived, sent, loads = gather_steps(nz, units, whole, send_sem, recv_sem, core_sem)
     slot_bufs = (grad, crecv, xa, yb, ya, xb, zbuf, zrecv)
     core_copy, stage_a, stage_b, stage_c, stage_d = scatter_steps(nz, MIXED, slot_bufs, rs_send, rs_recv, rs_out)
     small_stage = small_steps(nz, small, sbuf, srecv, szrecv, small_out, small_send, small_recv)
     pieces = len(MIXED) * PARTS
 
     def scatter(n):
-        if n + 1 < pieces:
+        if n + 1 < pieces and (n + 1) % PARTS:
             core_copy(n + 1).start()
         if n < pieces:
             stage_a(n)
@@ -671,7 +668,7 @@
             stage_b(n - 1)
         if 2 <= n < pieces + 2:
             stage_c(n - 2)
-        if n >= 3:
+        if 3 <= n < pieces + 3:
             stage_d(n - 3)
 
     def bias_copy(k, sending):
@@ -684,14 +681,13 @@
             device_id_type=MESH,
         )
 
-    def fetch(u, dst, turn=0, wait=True):
-        if turn == 0:
-            arrived(u)
-        for c in loads(u, dst, w_sem.at[u + turn]):
+    def fetch(u, dst):
+        arrived(u)
+        for c in loads(u, dst, w_sem.at[u]):
             c.start()
 
-    def ready(u, dst, turn=0):
-        for c in loads(u, dst, w_sem.at[u + turn]):
+    def ready(u, dst):
+        for c in loads(u, dst, w_sem.at[u]):
             c.wait()
 
     cot = dctx
@@ -733,7 +729,7 @@
             total = total + bias_all[k]
         bias_ref[...] = total
 
-    w_self, w_in, w_out = (wb0, wb1), (wb2, wb2), (wb1, wb0)
+    w_self, w_in, w_out = (wb3, wb1), (wb2, wb2), (wb1, wb3)
     u_self, u_in, u_out = (SELF0, SELF1), (IN0, IN1), (OUT0, OUT1)
 
     def cross_project_all():
@@ -792,19 +788,18 @@
         add_products(res, res, rows[s], hid, 3, w_self[s], False)
 
     def cross_in():
-        ready(CROSS, wb1, 7)
         norm_back(0, rw + rv, res, hat1, rstd1, vec, 1, nb, small, 2)
-        context_grad(nb, every, wb1, dctx)
-
-    def cross_back(s):
-        attend_back(qkv_c, dctx, (p_c0, p_c1)[s], slope, start[s], lens[s], start[1 - s], lens[1 - s])
+        context_grad(nb, every, wb0, dctx)
+
+    def cross_back(s, first, last):
+        attend_back(qkv_c, dctx, (p_c0, p_c1)[s], slope, start[s], lens[s], start[1 - s], lens[1 - s], first, last)
 
     def cross_sums():
         bias_sums(slope, every, rw + rv, small, 0, 1, False)
         small_stage(0)
 
     def finish_rows():
-        add_products(res, res, every, slope, 3, wb1, False)
+        add_products(res, res, every, slope, 3, wb0, False)
 
     def grads(m):
         if m < 6:
@@ -813,6 +808,7 @@
                 turned, src, right = ((t1, db, hid), (t2, nb, slope))[m % 3]
                 transpose_into(turned, src, start[s], count[s])
                 grad_tiles(grad, m, turned, count[s], right, rows[s], 0, nz, 0, True)
+                core_copy(m * PARTS).start()
                 return
             src, at, n, back, ctx, dqkv, dz = mb, start[s], count[s], rows[s], ctx_s, hid, db
         else:
@@ -821,6 +817,7 @@
         transpose_into(t2, src, at, n)
         grad_tiles(grad, m, t2, n, dqkv, back, 0, 3, 0, True)
         grad_tiles(grad, m, t1, n, ctx, back, 0, 1, 3 * D, False)
+        core_copy(m * PARTS).start()
 
     for k in range(1, nz):
         z_send(0, k)
@@ -846,83 +843,83 @@
     gather(10)
     fetch(IN1, wb2)
     self_norm(1)
-    cross_forward(0)
     gather(11)
     forward(1, 0, 2)
-    cross_norm(0)
     gather(12)
     forward(1, 2, nz)
     gather(13)
-    fetch(OUT1, wb0)
+    fetch(OUT1, wb3)
+    gather(14)
     out_rows(1)
     norm3(1)
-    gather(14)
     grads(0)
-    core_copy(0).start()
+    gather(15)
     du(1)
     scatter(0)
-    gather(15)
-    grads(1)
+    gather(16)
+    fetch(SELF0, wb3)
+    dn(1)
     scatter(1)
-    gather(16)
-    fetch(SELF0, wb0)
-    dn(1)
+    gather(17)
     self_in(1)
     scatter(2)
-    gather(17)
+    grads(1)
+    gather(18)
     self_back(1, 0, 3)
     scatter(3)
-    gather(18)
+    gather(19)
+    fetch(IN0, wb2)
     self_back(1, 3, 6)
     scatter(4)
-    gather(19)
-    fetch(IN0, wb2)
+    gather(20)
     dm(1)
     self_sums(1)
+    scatter(5)
     grads(2)
-    scatter(5)
-    gather(20)
+    gather(21)
+    cross_forward(0)
+    scatter(6)
+    gather(22)
+    fetch(OUT0, wb1)
+    cross_norm(0)
     self_project(0)
     self_forward(0)
-    scatter(6)
-    gather(21)
+    scatter(7)
     self_norm(0)
     forward(0, 0, nz)
-    scatter(7)
-    gather(22)
-    fetch(OUT0, wb1)
     out_rows(0)
     norm3(0)
+    scatter(8)
     grads(3)
-    scatter(8)
     du(0)
-    fetch(CROSS, wb1, 7)
     scatter(9)
     dn(0)
+    self_in(0)
     scatter(10)
+    self_back(0, 0, 6)
+    scatter(11)
     grads(4)
-    scatter(11)
-    self_in(0)
-    self_back(0, 0, 6)
-    scatter(12)
     dm(0)
     cross_in()
+    scatter(12)
+    cross_back(0, 0, 3)
     scatter(13)
+    cross_back(0, 3, 6)
+    scatter(14)
     self_sums(0)
     grads(5)
-    scatter(14)
-    cross_back(0)
+    cross_back(1, 0, 3)
     scatter(15)
-    cross_back(1)
+    cross_back(1, 3, 6)
     scatter(16)
+    cross_sums()
+    scatter(17)
     grads(6)
-    scatter(17)
-    cross_sums()
     scatter(18)
     small_stage(1)
-    finish_rows()
     scatter(19)
     small_stage(2)
+    finish_rows()
     scatter(20)
     small_stage(3)
     scatter(21)
@@ -956,6 +953,7 @@
         in_specs=[any_spec] * 6 + [smem] * 3 + [vmem] * 16,
         out_specs=[any_spec] * 7 + [vmem] * 4,
         scratch_shapes=[
+            vm((4, D, D), BF),
             vm((4, D, D), BF),
             vm((4, D, D), BF),
             vm((4, D, D), BF),
@@ -982,8 +980,8 @@
             vm((D, rows), BF),
             vm((D, rows), BF),
             vm((32, D), F32),
-            vm((2, 2, 2, 2, size * PARTS, width), BF),
-            vm((SLOTS, 2, 2, size, width), BF),
+            vm((2, 2, 2, size * PARTS, width), BF),
+            vm((CORE_SLOTS, 2, 2, size, width), BF),
             vm((SLOTS, 2, size, width // 2), BF),
             vm((SLOTS, 2, size, width // 2), BF),
             vm((SLOTS, size, width // 2), BF),
@@ -1002,13 +1000,14 @@
             vm((2, lv, lw), F32),
             vm((2, lw, lw), F32),
             vm((2, lv, lv), F32),
-            dma((7, nz - 1, K_Z2 + 1)),
-            dma((7, nz - 1, K_Z2 + 1)),
-            dma((8, nz + 1)),
+            dma((7,)),
+            dma((7, nz - 1, K_C)),
+            dma((7,)),
+            dma((7, nz + 1)),
             dma((nz,)),
             dma((nz,)),
-            dma((SLOTS, 4 + nz)),
-            dma((SLOTS, 4 + nz)),
+            dma((CORE_SLOTS, 4 + nz)),
+            dma((CORE_SLOTS, 4 + nz)),
             dma((2 + nz,)),
             dma((2 + nz,)),
         ],
@@ -1018,7 +1017,7 @@
     return outs[7:]
 
 
-VMEM_BYTES = 62 << 20
+VMEM_BYTES = 63 << 20
 
 
 def finish_kernel(es, nz, slots, *refs):
@@ -1092,7 +1091,7 @@
         in_specs=[pl.BlockSpec(memory_space=pltpu.HBM)] * 4,
         out_specs=[vmem] * len(shapes),
         scratch_shapes=[pltpu.VMEM(v.shape, v.dtype) for v in (sums, small, result, dinput)] + [pltpu.SemaphoreType.DMA((4,))],
-        compiler_params=pltpu.CompilerParams(vmem_limit_bytes=40 << 20),
+        compiler_params=pltpu.CompilerParams(vmem_limit_bytes=VMEM_BYTES),
         name="finish",
     )(sums, small, result, dinput)
 

time: 334 us -> 322 us (0.964)
  Pallas kernels: 328 us -> 321 us
  local copies, waits for them, and re-layouts: 4.9 us -> 0 us
    pallas_call x1, Pallas kernels: 325 us -> 316 us  [layer(): pl.pallas_call(functools.partial(layer_kernel, nz, lens), out_shape=[sd((...]
    unnamed x8 -> x0, local copies, waits for them, and re-layouts: 4.9 us -> none
where the time goes in v1:
time: 322 us; the launch traced here: 321 us
  Pallas kernels  321 us (100%)
    pallas_call x1, Pallas kernels, layer(): pl.pallas_call(functools.partial(layer_kernel, nz, lens), out_shape=[sd((...  316 us

profile of v1, /device:TPU:0, one launch (start us, length us, event | category | flops | bytes accessed | tf_op | source)
XLA Modules:
  0.0 321.4 jit_solution(35074013137188432)
XLA Ops:
  0.7 316.0 %layer.1 = (bf16[4,768,768]{2,1,0:T(8,128)(2,1)}, bf16[4,768,768]{2,1,0:T(8,128)(2,1)}, bf16[4,768,768]{2,1,0:T(8,128)(2,1)}, bf16[4,768,768]{2,1,0:T(8,128)(2,1...) custom-call(bf16[3,192,768]{2,1,0:T(8,128)(2,1)} %bitcast.15, ...), custom_call_target="tpu_custom_call" | custom-call | tf_op jit(solution)/shard_map/layer/pallas_call | solution.py:949
  316.7 4.5 %finish.1 = (bf16[20,8,768]{2,1,0:T(8,128)(2,1)}, bf16[36,8,768]{2,1,0:T(8,128)(2,1)}, f32[20,8,768]{2,1,0:T(8,128)}, f32[36,8,768]{2,1,0:T(8,128)}, f32[3,96,19...) custom-call(f32[7,3,32,768]{3,2,1,0:T(8,128)} %bitcast.13, ...), custom_call_target="tpu_custom_call" | custom-call | tf_op jit(solution)/shard_map/finish/pallas_call | solution.py:1088

commit v2 on v1

--- a/solution.py
+++ b/solution.py
@@ -273,7 +273,7 @@
 
 
 SLOTS = 4
-CORE_SLOTS = 7
+CORE_SLOTS = 6
 PARTS = 3
 
 
@@ -332,7 +332,7 @@
             merge(crecv.at[i % CORE_SLOTS, j // 2, j % 2], mine.at[j // 2, j % 2])
             return carry
 
-        lax.fori_loop(0, 4, body, 0)
+        lax.fori_loop(0, 4, body, 0, unroll=2)
         xa_copy(i).start()
         yb_copy(i).start()
 
@@ -346,7 +346,7 @@
             merge(crecv.at[i % CORE_SLOTS, by, j, :, hi], yb.at[s, j])
             return carry
 
-        lax.fori_loop(0, 2, body, 0)
+        lax.fori_loop(0, 2, body, 0, unroll=2)
         ya_copy(i).start()
         xb_copy(i).start()
 
@@ -598,7 +598,7 @@
         grad_ref[:, :, :, :, lanes] = y.reshape(2, 2, 2, size, TILE)
         return carry
 
-    lax.fori_loop(first * tiles, last * tiles, body, 0)
+    lax.fori_loop(first * tiles, last * tiles, body, 0, unroll=3)
 
 
 CROSS, SELF1, IN1, OUT1, SELF0, IN0, OUT0 = range(7)

time: 322 us -> 315 us (0.978)
  Pallas kernels: 321 us -> 314 us
    pallas_call x1, Pallas kernels: 316 us -> 310 us  [layer(): pl.pallas_call(functools.partial(layer_kernel, nz, lens), out_shape=[sd((...]
where the time goes in v2:
time: 315 us
  Pallas kernels  314 us (100%)
    pallas_call x1, Pallas kernels, layer(): pl.pallas_call(functools.partial(layer_kernel, nz, lens), out_shape=[sd((...  310 us

profile of v2, /device:TPU:0, one launch (start us, length us, event | category | flops | bytes accessed | tf_op | source)
XLA Modules:
  0.0 314.9 jit_solution(16279582213993811017)
XLA Ops:
  0.7 309.5 %layer.1 = (bf16[4,768,768]{2,1,0:T(8,128)(2,1)}, bf16[4,768,768]{2,1,0:T(8,128)(2,1)}, bf16[4,768,768]{2,1,0:T(8,128)(2,1)}, bf16[4,768,768]{2,1,0:T(8,128)(2,1...) custom-call(bf16[3,192,768]{2,1,0:T(8,128)(2,1)} %bitcast.15, ...), custom_call_target="tpu_custom_call" | custom-call | tf_op jit(solution)/shard_map/layer/pallas_call | solution.py:949
  310.2 4.5 %finish.1 = (bf16[20,8,768]{2,1,0:T(8,128)(2,1)}, bf16[36,8,768]{2,1,0:T(8,128)(2,1)}, f32[20,8,768]{2,1,0:T(8,128)}, f32[36,8,768]{2,1,0:T(8,128)}, f32[3,96,19...) custom-call(f32[7,3,32,768]{3,2,1,0:T(8,128)} %bitcast.13, ...), custom_call_target="tpu_custom_call" | custom-call | tf_op jit(solution)/shard_map/finish/pallas_call | solution.py:1088

commit v3 on v2

--- a/solution.py
+++ b/solution.py
@@ -182,7 +182,7 @@
         out_ref[c, xrows, at] = (y + bias_ref[pl.ds(b0 + c, 1), at]).astype(BF)
         return carry
 
-    lax.fori_loop(0, 3 * tiles, body, 0)
+    lax.fori_loop(0, 3 * tiles, body, 0, unroll=3)
 
 
 def half_lanes():
@@ -209,7 +209,7 @@
             ctx_ref[qr, lanes] = jnp.where(first, parts[0], parts[1]).astype(BF)
         return carry
 
-    lax.fori_loop(0, D // (2 * HEAD_DIM), body, 0, unroll=2)
+    lax.fori_loop(0, D // (2 * HEAD_DIM), body, 0, unroll=3)
 
 
 def out_norm(ctx_ref, start, count, w_ref, wi, resid_ref, vec_ref, v0, pre_ref, hat_ref, rstd_ref, full_ref, low_ref):
@@ -522,7 +522,7 @@
         small[pl.ds(row + zb, 1), at] = jnp.sum(eighth(du.astype(F32)), axis=0, keepdims=True)
         return carry
 
-    lax.fori_loop(0, slope_ref.shape[0] * tiles, body, 0)
+    lax.fori_loop(0, slope_ref.shape[0] * tiles, body, 0, unroll=2)
 
 
 def add_products(res_ref, out_ref, rows, x_ref, count, w_ref, transposed):
@@ -912,14 +912,14 @@
     scatter(15)
     cross_back(1, 3, 6)
     scatter(16)
-    cross_sums()
     scatter(17)
     grads(6)
+    cross_sums()
+    finish_rows()
     scatter(18)
     small_stage(1)
     scatter(19)
     small_stage(2)
-    finish_rows()
     scatter(20)
     small_stage(3)
     scatter(21)

time: 315 us -> 314 us (level)
  no operation moved by 1% of the time
where the time goes in v3:
time: 314 us
  Pallas kernels  313 us (100%)
    pallas_call x1, Pallas kernels, layer(): pl.pallas_call(functools.partial(layer_kernel, nz, lens), out_shape=[sd((...  309 us

profile of v3, /device:TPU:0, one launch (start us, length us, event | category | flops | bytes accessed | tf_op | source)
XLA Modules:
  0.0 314.2 jit_solution(4414270870922898815)
XLA Ops:
  0.7 308.8 %layer.1 = (bf16[4,768,768]{2,1,0:T(8,128)(2,1)}, bf16[4,768,768]{2,1,0:T(8,128)(2,1)}, bf16[4,768,768]{2,1,0:T(8,128)(2,1)}, bf16[4,768,768]{2,1,0:T(8,128)(2,1...) custom-call(bf16[3,192,768]{2,1,0:T(8,128)(2,1)} %bitcast.15, ...), custom_call_target="tpu_custom_call" | custom-call | tf_op jit(solution)/shard_map/layer/pallas_call | solution.py:949
  309.4 4.5 %finish.1 = (bf16[20,8,768]{2,1,0:T(8,128)(2,1)}, bf16[36,8,768]{2,1,0:T(8,128)(2,1)}, f32[20,8,768]{2,1,0:T(8,128)}, f32[36,8,768]{2,1,0:T(8,128)}, f32[3,96,19...) custom-call(f32[7,3,32,768]{3,2,1,0:T(8,128)} %bitcast.13, ...), custom_call_target="tpu_custom_call" | custom-call | tf_op jit(solution)/shard_map/finish/pallas_call | solution.py:1088
